TPU v7x, 512 devices: a whole 4x4x16 slice. The times are simulated.
512 devices in a mesh: row: 16 (over y, z_hi), col: 32 (over z_lo, x, core).
Axes of the slice: x: 4, y: 4, z: 16 (z_hi: 4, z_lo: 4; z = z_hi * 4 + z_lo), core: 2. Of those that a mesh axis runs over, the one named last changes fastest.
Arguments:
- normals: float32 [12288, 12288], P('row', 'col'), may hold values from -1 to 4, as said below
- design: float32 [512, 12288], P('row', 'col'), may hold values from -0.25 to 0.25
- filter_blocks: float32 [2, 32, 32], replicated, may hold values from -4 to 4, as said below
- regular: float32 [12288], replicated, may hold values from 0.1 to 1
Outputs:
- factored: float32 [12288, 12288], P('row', 'col')
Inputs may be any that keep to these rules, and one draw needn't show every extreme that they name: normals is symmetric; each diagonal entry is at least 1 and each off-diagonal entry has magnitude at most 1 / 256. filter_blocks[0][i, j] = f[i - j] for i >= j and 0 above the diagonal; filter_blocks[1][i, j] = f[32 + i - j] for j >= i and 0 below; f holds the 33 taps of one causal filter with f[0] at least 1.
All inputs are finite; a program needn't handle non-finite values.
Results may differ from a plain program's by a relative error of at most 0.00007.
Values sent between devices are 32-bit elements; how exact they have to be, the bound alone decides.
A program may use at most 64 MiB of HBM per device.

v0:
```python
import jax
import jax.numpy as jnp
from jax import lax
from jax.sharding import PartitionSpec as P

B = 256
P_SIZE = 32


def passed_along(value, axis, by):
    peers = lax.axis_size(axis)
    pairs = [(i, i + by) for i in range(peers) if 0 <= i + by < peers]
    return lax.ppermute(value, axis, pairs)


def broadcast(block, axis, holder):
    block = jnp.where(lax.axis_index(axis) == holder, block, jnp.zeros_like(block))
    return lax.psum(block, axis)


def contract_rows(left_side, right_side):
    return lax.dot_general(
        left_side,
        right_side,
        (((0,), (0,)), ((), ())),
        precision=lax.Precision.HIGHEST,
        preferred_element_type=jnp.float32,
    )


def body(normals, design, filter_blocks, regular):
    highest = lax.Precision.HIGHEST
    rows_here, cols_here = normals.shape
    obs_here = design.shape[0]
    row_index = lax.axis_index("row")
    col_index = lax.axis_index("col")
    tiles_per_row = lax.axis_size("col") // lax.axis_size("row")
    prior_rows = passed_along(design, "row", 1)
    blocks = design.reshape(obs_here // P_SIZE, P_SIZE, cols_here)
    before = jnp.concatenate([prior_rows[None], blocks[:-1]], axis=0)
    filtered = jnp.einsum("ij,bjc->bic", filter_blocks[0], blocks, precision=highest)
    filtered = filtered + jnp.einsum("ij,bjc->bic", filter_blocks[1], before, precision=highest)
    filtered = filtered.reshape(obs_here, cols_here)
    columns = lax.all_gather(filtered, "row", axis=0, tiled=True)
    pieces = [
        broadcast(columns, "col", row_index * tiles_per_row + offset)
        for offset in range(tiles_per_row)
    ]
    left_side = jnp.concatenate(pieces, axis=1)
    gram_tile = contract_rows(left_side, columns)
    row_pos = row_index * rows_here + jnp.arange(rows_here, dtype=jnp.int32)
    col_pos = col_index * cols_here + jnp.arange(cols_here, dtype=jnp.int32)
    reg_rows = lax.dynamic_slice_in_dim(regular, row_index * rows_here, rows_here)
    system = normals + gram_tile
    system = system + jnp.where(row_pos[:, None] == col_pos[None, :], reg_rows[:, None], 0.0)
    top_strip = broadcast(system[:B], "row", 0)
    corner = broadcast(top_strip[:, :B], "col", 0)
    factor = jnp.linalg.cholesky(corner)
    inverse = jax.scipy.linalg.solve_triangular(factor, jnp.eye(B, dtype=jnp.float32), lower=True)
    col_panel = lax.dot_general(
        top_strip,
        inverse,
        (((0,), (1,)), ((), ())),
        precision=highest,
        preferred_element_type=jnp.float32,
    )
    shares = [
        broadcast(col_panel, "col", row_index * tiles_per_row + offset)
        for offset in range(tiles_per_row)
    ]
    row_panel = jnp.concatenate(shares, axis=0)
    update = lax.dot_general(
        row_panel,
        col_panel,
        (((1,), (1,)), ((), ())),
        precision=highest,
        preferred_element_type=jnp.float32,
    )
    trailing = system - update
    padded = jnp.pad(row_panel, ((0, 0), (0, cols_here - B)))
    return jnp.where(col_pos[None, :] < B, padded, trailing)


def solution(mesh):
    in_specs = (P("row", "col"), P("row", "col"), P(), P())
    out_specs = P("row", "col")
    return jax.shard_map(body, mesh=mesh, in_specs=in_specs, out_specs=out_specs, check_vma=False)
```

profile of v0, /device:TPU:24, one launch (start us, length us, event | category | flops | bytes accessed | tf_op | source)
XLA Modules:
  0.0 1245.4 jit_solution(5678547278901079567)
XLA Ops:
  6.5 9.1 collective-permute-start
  15.6 1.0 fusion.26
  16.6 5.2 collective-permute-done
  21.9 0.9 fusion.11
  22.8 58.6 %all-gather = f32[1,512,384]{2,1,0:T(8,128)S(1)} all-gather(f32[1,32,384]{2,1,0:T(8,128)S(1)} %fusion.11), channel_id=2, replica_groups=mesh['row'=16,'col'=32] {'row'}, dimensions={1}, use_global_device_ids=true | all-gather | bytes 835584 | tf_op jit(solution)/shard_map/all_gather | solution.py:44
  81.4 1.3 bitcast_select_fusion.1
  82.7 1.2 copy-done
  84.3 0.8 dynamic_slice.3
  85.0 298.6 %all-reduce.15.cloned.1.call-done = (f32[512,384]{1,0:T(8,128)}, f32[512,384]{1,0:T(8,128)}) async-done(((f32[512,384]{1,0:T(8,128)}, f32[512,384]{1,0:T(8,128)}), (f32[512,384]{1,0:T(8,128)}, f32[512,384]{1,0:T(8,128)})) %all-reduce.15.cloned.1.call-update) | async-done | bytes 1572880 | tf_op jit(solution)/shard_map/psum | solution.py:18
  383.7 3.6 fusion.7
  387.3 0.8 slice_select_fusion
  388.1 203.7 %all-reduce.9.cloned.1.call-done = f32[256,384]{0,1:T(8,128)} async-done(((f32[256,384]{0,1:T(8,128)}), f32[256,384]{0,1:T(8,128)}) %all-reduce.9.cloned.1.call-update) | async-done | bytes 393232 | tf_op jit(solution)/shard_map/psum | solution.py:18
  591.8 1.7 slice_select_fusion.1
  593.8 286.1 %all-reduce.11.cloned.1.call-done = f32[256,256]{0,1:T(8,128)} async-done(((f32[256,256]{0,1:T(8,128)}), f32[256,256]{0,1:T(8,128)}) %all-reduce.11.cloned.1.call-update) | async-done | bytes 262160 | tf_op jit(solution)/shard_map/psum | solution.py:18
  879.9 1.1 copy.7
  881.0 1.0 fusion.17
  882.0 11.7 cholesky.49
  893.7 9.8 custom-call.15
  904.0 11.7 cholesky.103
  916.1 0.7 compare_reduce_fusion
  918.3 4.5 while.1
  918.5 0.6 fusion.43
  919.1 1.4 dynamic-slice.7
  920.7 0.6 fusion.43
  921.3 1.4 dynamic-slice.7
  922.8 19.7 %custom-call.16 = f32[2,128,128]{1,2,0:T(8,128)S(1)} custom-call(f32[2,128,128]{2,1,0:T(8,128)S(1)} %get-tuple-element.12), custom_call_target="InvertDiagBlocksLowerTriangular" | custom-call | tf_op jit(solution)/shard_map/jit(_solve_triangular)/triangular_solve | solution.py:59
  944.1 0.9 broadcast_select_fusion
  945.1 289.1 %all-reduce.13.cloned.1.call-done = (f32[384,256]{0,1:T(8,128)}, f32[384,256]{0,1:T(8,128)}) async-done(((f32[384,256]{0,1:T(8,128)}, f32[384,256]{0,1:T(8,128)}), (f32[384,256]{0,1:T(8,128)}, f32[384,256]{0,1:T(8,128)})) %all-reduce.13.cloned.1.call-update) | async-done | bytes 786448 | tf_op jit(solution)/shard_map/psum | solution.py:18
  1234.2 1.0 constant_dynamic-update-slice_fusion.1
  1235.2 1.0 constant_dynamic-update-slice_fusion
  1236.3 1.2 fusion.10
  1237.5 1.4 copy.15
  (42 shorter events, 3.5 us)
Async XLA Ops:
  6.5 377.1 %all-reduce.15.cloned.1.call-start = ((), (), s32[]{:S(2)}) async-start(), calls=%async_computation.3 | async-start | bytes 3145728 | tf_op jit(solution)/shard_map/psum | solution.py:18
  6.5 15.3 %collective-permute-start = (f32[32,384]{1,0:T(8,128)}, f32[32,384]{1,0:T(8,128)S(1)}, u32[]{:S(2)}, u32[]{:S(2)}) collective-permute-start(f32[32,384]{1,0:T(8,128)} %param.5), channel_id=1, source_target_pairs={{0,32},{32,64},{64,96},{96,128},{128,160},{160,192},{192,224},{224... | collective-permute-start | bytes 147464 | tf_op jit(solution)/shard_map/ppermute | solution.py:13
  82.6 1.3 copy-start
  82.6 509.2 %all-reduce.9.cloned.1.call-start = ((), (), s32[]{:S(2)}) async-start(), calls=%async_computation | async-start | bytes 786432 | tf_op jit(solution)/shard_map/psum | solution.py:18
  388.1 491.8 %all-reduce.11.cloned.1.call-start = ((), (), s32[]{:S(2)}) async-start(), calls=%async_computation.1 | async-start | bytes 524288 | tf_op jit(solution)/shard_map/psum | solution.py:18
  593.5 640.7 %all-reduce.13.cloned.1.call-start = ((), (), s32[]{:S(2)}) async-start(), calls=%async_computation.2 | async-start | bytes 1572864 | tf_op jit(solution)/shard_map/psum | solution.py:18
  918.3 25.1 %copy-start.1 = (f32[256,384]{0,1:T(8,128)S(1)}, f32[256,384]{0,1:T(8,128)}, u32[]{:S(2)}) copy-start(f32[256,384]{0,1:T(8,128)} %all-reduce.9.cloned.1.call-done) | copy-start | bytes 1179652
Sparse Core Ops, SparseCore 0:
  82.8 300.8 all-reduce.14
  388.2 203.5 all-reduce.8
  594.7 285.1 all-reduce.10
  945.2 288.9 all-reduce.12
where the time goes:
time: 1250 us
  waiting for transfers between devices  1080 us (86%)
  other arithmetic  59.4 us (5%)
  blocking collectives  58.6 us (5%)
  between operations  14.7 us (1%)
    psum x4, waiting for transfers between devices, broadcast(): return lax.psum(block, axis)  1080 us
    all_gather x1, blocking collectives, body(): columns = lax.all_gather(filtered, 'row', axis=0, tiled=True)  58.6 us
    another operation x6, other arithmetic, body(): factor = jnp.linalg.cholesky(corner)  34 us
  transfers between devices with their start and end apart: 5, of which 5 were waited for; matrix products, arithmetic and copies ran while one was open for 0% of the time, Pallas kernels for 0%

commit v1 on v0

v1 whole, which is shorter than its diff:
```python
import functools

import jax
import jax.numpy as jnp
from jax import lax
from jax.experimental import pallas as pl
from jax.experimental.pallas import tpu as pltpu
from jax.sharding import PartitionSpec as P

B = 256
P_SIZE = 32
OBS = 512
MESH = pl.DeviceIdType.MESH
VMEM = pltpu.VMEM
HIGHEST = lax.Precision.HIGHEST

DK, D0, NK, N0, DR, NR = range(6)


def comm_kernel(design, normals, dk, dr, d0, nk, nr, n0, ssem, rsem, xsem, psem, qsem, lsem):
    row = lax.axis_index("row")
    col = lax.axis_index("col")
    s = lax.rem(col, 2)
    k = lax.div(col, 2)
    x, zl = lax.rem(k, 4), lax.div(k, 4)
    y, zh = lax.div(row, 4), lax.rem(row, 4)

    def at(y_=None, zh_=None, zl_=None, x_=None, s_=None):
        y_ = y if y_ is None else lax.rem(y_ + 4, 4)
        zh_ = zh if zh_ is None else lax.rem(zh_ + 4, 4)
        zl_ = zl if zl_ is None else lax.rem(zl_ + 4, 4)
        x_ = x if x_ is None else lax.rem(x_ + 4, 4)
        s_ = s if s_ is None else s_
        return (4 * y_ + zh_, 8 * zl_ + 2 * x_ + s_)

    def rslot(y_, zh_):
        return 4 * lax.rem(y_ + 4, 4) + lax.rem(zh_ + 4, 4)

    def kslot(zl_, x_):
        return 4 * lax.rem(zl_ + 4, 4) + lax.rem(x_ + 4, 4)

    flip = (k, 2 * row + s)
    off_diag = k != row
    partner = at(s_=1 - s)

    barrier = pltpu.get_barrier_semaphore()

    def hello(device):
        pl.semaphore_signal(barrier, inc=1, device_id=device, device_id_type=MESH)

    near = [at(zh_=zh + 1), at(zh_=zh - 1), at(y_=y + 1), at(y_=y - 1), at(x_=x + 1), at(x_=x - 1)]
    near += [at(zl_=zl + 1), at(zl_=zl + 2), at(zl_=zl + 3), partner]
    for device in near:
        hello(device)

    @pl.when(off_diag)
    def _():
        hello(flip)

    @pl.when(row != 0)
    def _():
        hello((0, col))

    @pl.when(col != 0)
    def _():
        hello((row, 0))

    bufs = {DK: dk, D0: d0.at[s], NK: nk, N0: n0.at[s], DR: dr.at[s], NR: nr.at[s]}

    own = pltpu.make_async_copy(design, dk.at[row], lsem.at[0])
    own.start()
    own_strip = pltpu.make_async_copy(normals.at[pl.ds(0, 16), :], nk.at[0], lsem.at[1])
    own_corner = pltpu.make_async_copy(design.at[:, pl.ds(0, 128)], d0.at[0, row], lsem.at[2])
    own_flip = pltpu.make_async_copy(design, dr.at[s, k], lsem.at[3])

    @pl.when(row == 0)
    def _():
        own_strip.start()

    @pl.when(col == 0)
    def _():
        own_corner.start()

    @pl.when(k == row)
    def _():
        own_flip.start()

    one = jnp.int32(1)
    count = len(near) + jnp.where(off_diag, one, 0) + jnp.where(row == 0, 15 * one, 0) + jnp.where(col == 0, 31 * one, 0)
    pl.semaphore_wait(barrier, count)

    def send(flow, slot, device, half=None, src=None):
        buf = bufs[flow]
        rows = buf.shape[1]
        if half is None:
            part = buf.at[slot]
        else:
            part = buf.at[slot, pl.ds(half * (rows // 2), rows // 2), :]
        pltpu.make_async_remote_copy(
            src_ref=part if src is None else src,
            dst_ref=part,
            send_sem=ssem.at[flow],
            recv_sem=rsem.at[flow, slot],
            device_id=device,
            device_id_type=MESH,
        ).start()

    def arrived(flow, slot):
        buf = bufs[flow]
        pltpu.make_async_remote_copy(
            src_ref=buf.at[slot],
            dst_ref=buf.at[slot],
            send_sem=ssem.at[flow],
            recv_sem=rsem.at[flow, slot],
            device_id=partner,
            device_id_type=MESH,
        ).wait_recv()

    def other(src, dst, send_sem, recv_sem, device):
        return pltpu.make_async_remote_copy(
            src_ref=src, dst_ref=dst, send_sem=send_sem, recv_sem=recv_sem, device_id=device, device_id_type=MESH
        )

    @pl.when(row == 0)
    def _():
        for t in range(1, 16):
            other(normals.at[pl.ds(16 * t, 16), :], nk.at[t], xsem.at[0], rsem.at[NK, t], (t, col)).start()

    def along_row(flow, source):
        full = d0 if flow == D0 else n0
        for t in range(1, 32):
            h = t % 2
            other(
                source.at[:, pl.ds(128 * h, 128)],
                full.at[h, row],
                xsem.at[(1 if flow == D0 else 3) + h],
                rsem.at[flow, row],
                (row, t),
            ).start()

    @pl.when(col == 0)
    def _():
        along_row(D0, design)

    def z_send(flow, src=None):
        slot = rslot(y, zh)
        send(flow, slot, at(zh_=zh + 1), src=src)
        send(flow, slot, at(zh_=zh - 1), src=src)

    def y_send(flow, zz, src=None):
        slot = rslot(y, zz)
        send(flow, slot, at(y_=y + 1), src=src)
        send(flow, slot, at(y_=y - 1), src=src)

    def z_down(flow):
        slot = rslot(y, zh - 1)
        arrived(flow, slot)
        send(flow, slot, at(zh_=zh + 1), half=0)
        y_send(flow, zh - 1)

    def z_up(flow):
        slot = rslot(y, zh + 1)
        arrived(flow, slot)
        send(flow, slot, at(zh_=zh - 1), half=1)
        y_send(flow, zh + 1)

    def z_far(flow):
        arrived(flow, rslot(y, zh + 2))
        y_send(flow, zh + 2)

    def y_near(flow, zz):
        slot = rslot(y - 1, zz)
        arrived(flow, slot)
        send(flow, slot, at(y_=y + 1), half=0)
        slot = rslot(y + 1, zz)
        arrived(flow, slot)
        send(flow, slot, at(y_=y - 1), half=1)

    def y_far(flow, zz):
        arrived(flow, rslot(y + 2, zz))

    def flip_send(flow, src, which):
        @pl.when(off_diag)
        def _():
            other(src, bufs[flow].at[row], xsem.at[which], rsem.at[flow, row], flip).start()

    def l_send(flow):
        slot = kslot(zl, x)
        for d in (1, 2, 3):
            send(flow, slot, at(zl_=zl + d))

    def x_send(flow, ll):
        slot = kslot(ll, x)
        send(flow, slot, at(x_=x + 1))
        send(flow, slot, at(x_=x - 1))

    def x_near(flow, ll):
        slot = kslot(ll, x - 1)
        arrived(flow, slot)
        send(flow, slot, at(x_=x + 1), half=0)
        slot = kslot(ll, x + 1)
        arrived(flow, slot)
        send(flow, slot, at(x_=x - 1), half=1)

    def x_far(flow, ll):
        arrived(flow, kslot(ll, x + 2))

    def share(flow, d):
        full = dr if flow == DR else nr
        first = 4 * lax.rem(zl + d, 4)
        part = full.at[s, pl.ds(first, 4)]
        return other(part, part, psem.at[flow - DR, d, 0], psem.at[flow - DR, d, 1], partner)

    def share_wait(flow, d):
        full = dr if flow == DR else nr
        first = 4 * lax.rem(zl + d, 4)
        part = full.at[1 - s, pl.ds(first, 4)]
        other(part, part, psem.at[flow - DR, d, 0], psem.at[flow - DR, d, 1], partner).wait_recv()

    def share_corner(flow):
        full, which = (d0, 0) if flow == D0 else (n0, 1)
        return other(full.at[s], full.at[s], qsem.at[which, 0], qsem.at[which, 1], partner)

    def share_corner_wait(flow):
        full, which = (d0, 0) if flow == D0 else (n0, 1)
        other(full.at[1 - s], full.at[1 - s], qsem.at[which, 0], qsem.at[which, 1], partner).wait_recv()

    z_send(DK, design)
    y_send(DK, zh, design)
    flip_send(DR, design, 5)
    own.wait()

    @pl.when(col != 0)
    def _():
        arrived(D0, row)

    @pl.when(col == 0)
    def _():
        own_corner.wait()

    z_send(D0)
    y_send(D0, zh)
    y_near(DK, zh)

    @pl.when(row != 0)
    def _():
        arrived(NK, row)

    @pl.when(row == 0)
    def _():
        own_strip.wait()

    @pl.when(col == 0)
    def _():
        along_row(N0, nk.at[row])
        pltpu.make_async_copy(nk.at[row, :, pl.ds(0, 128)], n0.at[0, row], lsem.at[4]).start()
        pltpu.make_async_copy(nk.at[row, :, pl.ds(0, 128)], n0.at[0, row], lsem.at[4]).wait()

    z_send(NK)
    y_send(NK, zh)
    flip_send(NR, nk.at[row], 6)
    z_down(DK)
    z_up(DK)
    y_near(D0, zh)
    z_down(D0)
    z_up(D0)

    @pl.when(col != 0)
    def _():
        arrived(N0, row)

    z_send(N0)
    y_send(N0, zh)

    @pl.when(off_diag)
    def _():
        arrived(DR, k)

    @pl.when(k == row)
    def _():
        own_flip.wait()

    l_send(DR)
    x_send(DR, zl)
    y_near(DK, zh - 1)
    y_near(DK, zh + 1)
    z_far(DK)
    z_far(D0)
    y_near(D0, zh - 1)
    y_near(D0, zh + 1)
    y_near(D0, zh + 2)
    y_near(DK, zh + 2)
    y_near(NK, zh)
    x_near(DR, zl)
    z_down(NK)
    z_up(NK)
    y_near(N0, zh)
    z_down(N0)
    z_up(N0)
    for d in (1, 3, 2):
        arrived(DR, kslot(zl + d, x))
        x_send(DR, zl + d)

    @pl.when(off_diag)
    def _():
        arrived(NR, k)

    @pl.when(k == row)
    def _():
        pltpu.make_async_copy(nk.at[row], nr.at[s, k], lsem.at[5]).start()
        pltpu.make_async_copy(nk.at[row], nr.at[s, k], lsem.at[5]).wait()

    l_send(NR)
    x_send(NR, zl)
    for zz in (-1, 1):
        y_near(NK, zh + zz)
        y_near(N0, zh + zz)
    z_far(N0)
    z_far(NK)
    x_far(DR, zl)
    share(DR, 0).start()
    for d in (1, 3, 2):
        x_near(DR, zl + d)
    y_near(N0, zh + 2)
    y_near(NK, zh + 2)
    x_near(NR, zl)
    for d in (1, 3, 2):
        arrived(NR, kslot(zl + d, x))
        x_send(NR, zl + d)
    for zz in (0, -1, 1, 2):
        y_far(D0, zh + zz)
    share_corner(D0).start()
    for zz in (0, -1, 1, 2):
        y_far(N0, zh + zz)
    share_corner(N0).start()
    for d in (1, 3, 2):
        x_far(DR, zl + d)
        share(DR, d).start()
    for d in (1, 3, 2):
        x_near(NR, zl + d)
    for d in (0, 1, 3, 2):
        x_far(NR, zl + d)
        share(NR, d).start()
    for zz in (0, -1, 1, 2):
        y_far(DK, zh + zz)
        y_far(NK, zh + zz)

    share_corner_wait(D0)
    share_corner_wait(N0)
    for d in range(4):
        share_wait(DR, (4 - 0 + d) % 4)
    for d in range(4):
        share_wait(NR, d)
    share_corner(D0).wait_send()
    share_corner(N0).wait_send()
    for d in range(4):
        share(DR, d).wait_send()
        share(NR, d).wait_send()
    for flow in range(6):
        part = bufs[flow].at[pl.ds(0, 15)]
        other(part, part, ssem.at[flow], rsem.at[flow, 0], partner).wait_send()

    @pl.when(off_diag)
    def _():
        other(design, design, xsem.at[5], rsem.at[DR, 0], partner).wait_send()
        other(nk.at[0], nk.at[0], xsem.at[6], rsem.at[NR, 0], partner).wait_send()

    @pl.when(row == 0)
    def _():
        part = nk.at[pl.ds(0, 15)]
        other(part, part, xsem.at[0], rsem.at[NK, 0], partner).wait_send()

    @pl.when(col == 0)
    def _():
        for full, first in ((d0, 1), (n0, 3)):
            part = full.at[0, pl.ds(0, 15)]
            other(part, part, xsem.at[first], rsem.at[D0, 0], partner).wait_send()
            other(full.at[1], full.at[1], xsem.at[first + 1], rsem.at[D0, 0], partner).wait_send()


def gather_all(design, normals):
    f32 = jnp.float32
    wide = design.shape[1]
    shapes = [
        (16, P_SIZE, wide),
        (2, 16, P_SIZE, wide),
        (2, 16, P_SIZE, 128),
        (16, 16, wide),
        (2, 16, 16, wide),
        (2, 16, 16, 128),
    ]
    dma = pltpu.SemaphoreType.DMA
    return pl.pallas_call(
        comm_kernel,
        out_shape=[jax.ShapeDtypeStruct(shape, f32) for shape in shapes],
        in_specs=[pl.BlockSpec(memory_space=VMEM), pl.BlockSpec(memory_space=pl.ANY)],
        out_specs=[pl.BlockSpec(memory_space=VMEM)] * 6,
        scratch_shapes=[dma((6,)), dma((6, 16)), dma((7,)), dma((2, 4, 2)), dma((2, 2)), dma((6,))],
        compiler_params=pltpu.CompilerParams(collective_id=0, has_side_effects=True),
    )(design, normals)


def dot(a, b, da=1, db=0, precision=HIGHEST):
    return lax.dot_general(a, b, (((da,), (db,)), ((), ())), precision=precision, preferred_element_type=jnp.float32)


def split(a):
    high = a.astype(jnp.bfloat16)
    return high, (a - high.astype(jnp.float32)).astype(jnp.bfloat16)


def dot3(a, b, da=0, db=0):
    (ah, al), (bh, bl) = a, b
    return dot(ah, bh, da, db, None) + (dot(ah, bl, da, db, None) + dot(al, bh, da, db, None))


def iota(shape, dim):
    return lax.broadcasted_iota(jnp.int32, shape, dim)


def inverse_factor(a, w, n, nb):
    w[...] = (iota((n, n), 0) == iota((n, n), 1)).astype(jnp.float32)
    for o in range(0, n, nb):
        e = o + nb
        eye = (iota((nb, nb), 0) == iota((nb, nb), 1)).astype(jnp.float32)
        m = jnp.concatenate([a[o:e, o:e], eye], axis=1)
        below = iota((nb, 1), 0)
        for t in range(nb - 1):
            pivot = m[t : t + 1, t : t + 1]
            scaled = m[t : t + 1, :] * (1.0 / pivot)
            weight = jnp.where(below > t, m[:, t : t + 1], 0.0)
            m = m - weight * scaled
        diag = jnp.sum(m[:, :nb] * eye, axis=1, keepdims=True)
        own = m[:, nb:] * (1.0 / jnp.sqrt(diag))
        left = dot(own, w[o:e, :e])
        w[o:e, :e] = left
        if e < n:
            right = dot(own, a[o:e, e:])
            a[e:, e:] -= dot(right, right, 0, 0)
            w[e:, :e] -= dot(right, left, 0, 0)


def compute_kernel(nb, normals, dk, dr, d0, nk, nr, n0, filters, regular, out, toeplitz, fk, fr, corner, inverse):
    row = lax.axis_index("row")
    col = lax.axis_index("col")
    rows, cols = normals.shape
    step = 4 * P_SIZE
    toeplitz[...] = jnp.zeros_like(toeplitz)
    for i in range(4):
        here = slice(P_SIZE * i, P_SIZE * (i + 1))
        toeplitz[here, P_SIZE * i : P_SIZE * (i + 1)] = filters[1]
        toeplitz[here, P_SIZE * (i + 1) : P_SIZE * (i + 2)] = filters[0]
    taps = toeplitz[...]

    def filtered(data):
        parts = [dot(taps[:, P_SIZE:], data[:step, :])]
        for o in range(step, OBS, step):
            parts.append(dot(taps, data[o - P_SIZE : o + step, :]))
        return jnp.concatenate(parts, axis=0)

    f0 = filtered(jnp.concatenate([d0[0], d0[1]], axis=1))
    reg0 = jnp.where(iota((B, B), 0) == iota((B, B), 1), regular[:, :B], 0.0)
    corner[...] = jnp.concatenate([n0[0], n0[1]], axis=1) + dot(f0, f0, 0, 0) + reg0
    inverse_factor(corner, inverse, B, nb)
    w = inverse[...]
    f0s = split(f0)
    fk[...] = filtered(dk)
    fks = split(fk[...])

    def strip(base, data, first, width):
        reg = regular[:, pl.ds(pl.multiple_of(first, 128), width)]
        same = iota((B, width), 0) == iota((B, width), 1) + first
        return base + dot3(f0s, data) + jnp.where(same, reg, 0.0)

    pk = dot(w, strip(nk[...], fks, cols * col, cols))
    pks = split(pk)
    half = rows // 2
    reg = regular[:, pl.ds(pl.multiple_of(cols * col, 128), cols)]
    for h in range(2):
        fr[...] = filtered(dr.at[h])
        frs = split(fr[...])
        first = row * rows + half * h
        side = strip(nr[h], frs, first, half)
        pr = dot(w, side)
        same = iota((half, cols), 0) + first == iota((half, cols), 1) + cols * col
        here = slice(half * h, half * (h + 1))
        tile = normals[here, :] + jnp.where(same, reg, 0.0) + dot3(frs, fks)
        out[here, :] = tile - dot3(split(pr), pks)

        @pl.when(col == 0)
        def _():
            out[here, :B] = dot(side, w, 0, 1)


def local_step(nb, normals, gathered, filters, regular):
    dk, dr, d0, nk, nr, n0 = gathered
    rows, cols = normals.shape
    f32 = jnp.float32
    return pl.pallas_call(
        functools.partial(compute_kernel, nb),
        out_shape=jax.ShapeDtypeStruct((rows, cols), f32),
        in_specs=[pl.BlockSpec(memory_space=VMEM)] * 9,
        out_specs=pl.BlockSpec(memory_space=VMEM),
        scratch_shapes=[
            VMEM((4 * P_SIZE, 5 * P_SIZE), f32),
            VMEM((OBS, cols), f32),
            VMEM((OBS, cols), f32),
            VMEM((B, B), f32),
            VMEM((B, B), f32),
        ],
    )(
        normals,
        dk.reshape(OBS, cols),
        dr.reshape(2, OBS, cols),
        d0.reshape(2, OBS, 128),
        nk.reshape(B, cols),
        nr.reshape(2, B, cols),
        n0.reshape(2, B, 128),
        filters,
        regular.reshape(1, -1),
    )


def body(normals, design, filter_blocks, regular):
    gathered = gather_all(design, normals)
    return local_step(64, normals, gathered, filter_blocks, regular)


def solution(mesh):
    in_specs = (P("row", "col"), P("row", "col"), P(), P())
    out_specs = P("row", "col")
    return jax.shard_map(body, mesh=mesh, in_specs=in_specs, out_specs=out_specs, check_vma=False)
```

time: 1250 us -> 118 us (0.09)
  the two profiles are of different devices: /device:TPU:24 before, /device:TPU:41 now
where the time goes in v1:
time: 118 us
  Pallas kernels  118 us (100%)
    pallas_call x1, Pallas kernels, gather_all(): pl.pallas_call(comm_kernel, out_shape=[jax.ShapeDtypeStruct(shape, f32) f...  81.7 us
    pallas_call x1, Pallas kernels, local_step(): pl.pallas_call(functools.partial(compute_kernel, nb), out_shape=jax.Shape...  36.4 us

profile of v1, /device:TPU:41, one launch (start us, length us, event | category | flops | bytes accessed | tf_op | source)
XLA Modules:
  0.0 118.2 jit_solution(9092345589141201537)
XLA Ops:
  0.0 81.7 %shard_map.46 = (f32[16,32,384]{2,1,0:T(8,128)}, f32[2,16,32,384]{3,2,1,0:T(8,128)}, f32[2,16,32,128]{3,2,1,0:T(8,128)}, f32[16,16,384]{2,1,0:T(8,128)}, f32[2,1...) custom-call(f32[32,384]{1,0:T(8,128)} %design.1, f32[768,384]{1,0:T(8,128)} %normals.3), custom_call_target="tpu_custom_call" | custom-call | tf_op jit(solution)/shard_map/pallas_call | solution.py:393
  81.8 36.4 %shard_map.47 = f32[768,384]{1,0:T(8,128)} custom-call(f32[768,384]{1,0:T(8,128)} %normals.3, f32[512,384]{1,0:T(8,128)} %bitcast.8, f32[2,512,384]{2,1,0:T(8,128)} %bitcast.7, f32[2,512,128]{2,1,0:T(8,128)} %bitcast.10, f32[256,384]{1,0:T(8,128)} %bitcast.11, f32[2,256,384]{2,1,0:T(8,128)} %bitcast.9, f32[2,256,128]{2,1,0:T(8,128)} %bitcast.12, ...), custom_call_target="tpu_custom_call" | custom-call | tf_op jit(solution)/shard_map/pallas_call | solution.py:499

commit v2 on v0

v2 whole, which is shorter than its diff:
```python
import functools

import jax
import jax.numpy as jnp
from jax import lax
from jax.experimental import pallas as pl
from jax.experimental.pallas import tpu as pltpu
from jax.sharding import PartitionSpec as P

B = 256
P_SIZE = 32
OBS = 512
MESH = pl.DeviceIdType.MESH
VMEM = pltpu.VMEM
HIGHEST = lax.Precision.HIGHEST

DK, D0, NK, N0, DR, NR, HOP = range(7)


def comm_kernel(design, normals, dk, dr, d0, nk, nr, n0, hop, ssem, rsem, xsem, psem, lsem):
    row = lax.axis_index("row")
    col = lax.axis_index("col")
    s = lax.rem(col, 2)
    k = lax.div(col, 2)
    x, zl = lax.rem(k, 4), lax.div(k, 4)
    y, zh = lax.div(row, 4), lax.rem(row, 4)

    def at(y_=None, zh_=None, zl_=None, x_=None, s_=None):
        y_ = y if y_ is None else lax.rem(y_ + 4, 4)
        zh_ = zh if zh_ is None else lax.rem(zh_ + 4, 4)
        zl_ = zl if zl_ is None else lax.rem(zl_ + 4, 4)
        x_ = x if x_ is None else lax.rem(x_ + 4, 4)
        s_ = s if s_ is None else s_
        return (4 * y_ + zh_, 8 * zl_ + 2 * x_ + s_)

    def slot_of(a, b):
        return 4 * lax.rem(a + 4, 4) + lax.rem(b + 4, 4)

    partner = at(s_=1 - s)
    top = row == 0
    side = col == 0
    home = zl == y
    source = zh == x

    barrier = pltpu.get_barrier_semaphore()

    def hello(device):
        pl.semaphore_signal(barrier, inc=1, device_id=device, device_id_type=MESH)

    near = [at(zh_=zh + 1), at(zh_=zh - 1), partner]
    for d in (1, 2, 3):
        near += [at(y_=y + d), at(x_=x + d), at(zl_=zl + d)]
    for device in near:
        hello(device)

    @pl.when(col != 0)
    def _():
        hello((row, 0))

    def copy(src, dst, which):
        return pltpu.make_async_copy(src, dst, lsem.at[which])

    own = copy(design, dk.at[row], 0)
    own.start()
    own_hop = copy(design, hop, 1)
    own_corner = copy(design.at[:, pl.ds(0, 128)], d0.at[0, row], 2)
    own_n0 = copy(normals.at[pl.ds(0, 8), pl.ds(0, B)], n0.at[0, 0], 3)
    own_nk = [copy(normals.at[pl.ds(32 * u, 32), :], nk.at[pl.ds(32 * u, 32), :], 4 + u) for u in range(2)]
    own_nr = [copy(normals.at[pl.ds(48 * u, 48), pl.ds(0, B)], nr.at[0, 0, pl.ds(48 * u, 48)], 6 + u) for u in range(2)]
    own_dr = copy(hop, dr.at[s, slot_of(y, x)], 8)

    @pl.when(source)
    def _():
        own_hop.start()

    @pl.when(top)
    def _():
        own_nk[0].start()
        own_nk[1].start()

    @pl.when(side)
    def _():
        own_corner.start()
        own_nr[0].start()
        own_nr[1].start()

    @pl.when(top & side)
    def _():
        own_n0.start()

    one = jnp.int32(1)
    pl.semaphore_wait(barrier, len(near) + jnp.where(side, 31 * one, 0))

    def remote(src, dst, send_sem, recv_sem, device):
        return pltpu.make_async_remote_copy(
            src_ref=src, dst_ref=dst, send_sem=send_sem, recv_sem=recv_sem, device_id=device, device_id_type=MESH
        )

    def sent(part, which):
        remote(part, part, xsem.at[which], rsem.at[DK, 0], partner).wait_send()

    bufs = {DK: dk, D0: d0.at[s], DR: dr.at[s]}

    def part_of(flow, slot, half=None):
        buf = bufs[flow]
        if half is None:
            return buf.at[slot]
        return buf.at[slot, pl.ds(16 * half, 16), :]

    def send(flow, slot, device, half=None, src=None, sem=None):
        part = part_of(flow, slot, half)
        sem = ssem.at[flow] if sem is None else sem
        remote(part if src is None else src, part, sem, rsem.at[flow, slot], device).start()

    def arrived(flow, slot):
        part = part_of(flow, slot)
        remote(part, part, ssem.at[flow], rsem.at[flow, slot], partner).wait_recv()

    @pl.when(side)
    def _():
        for t in range(1, 32):
            h = t % 2
            remote(design.at[:, pl.ds(128 * h, 128)], d0.at[h, row], xsem.at[h], rsem.at[D0, row], (row, t)).start()

    def n0_part(t):
        return normals.at[pl.ds(128 * (t % 2) + 8 * (t // 2), 8), pl.ds(0, B)]

    @pl.when(top & side)
    def _():
        for t in range(1, 32):
            h, q = t % 2, t // 2
            remote(n0_part(t), n0.at[h, q], xsem.at[2 + h], rsem.at[N0, q], (0, t)).start()

    def z_send(flow, src=None):
        slot = slot_of(y, zh)
        send(flow, slot, at(zh_=zh + 1), src=src)
        send(flow, slot, at(zh_=zh - 1), src=src)

    def y_send(flow, zz, src=None):
        slot = slot_of(y, zz)
        send(flow, slot, at(y_=y + 1), src=src)
        send(flow, slot, at(y_=y - 1), src=src)
        if flow == D0:
            send(flow, slot, at(y_=y + 2))

    def spread(d):
        @pl.when(source)
        def _():
            remote(dk.at[slot_of(y, zh + d)], hop, xsem.at[4], rsem.at[HOP, 0], at(x_=x + d)).start()

    def z_near(flow, d):
        slot = slot_of(y, zh + d)
        arrived(flow, slot)
        send(flow, slot, at(zh_=zh - d), half=0 if d < 0 else 1)
        if flow == DK:
            spread(d)
        y_send(flow, zh + d)

    def z_far(flow):
        arrived(flow, slot_of(y, zh + 2))
        if flow == DK:
            spread(2)
        y_send(flow, zh + 2)

    def y_near(flow, zz):
        for d in (-1, 1):
            slot = slot_of(y + d, zz)
            arrived(flow, slot)
            send(flow, slot, at(y_=y - d), half=0 if d < 0 else 1)

    def y_far(flow, zz):
        if flow == D0:
            arrived(flow, slot_of(y - 1, zz))
            arrived(flow, slot_of(y + 1, zz))
        arrived(flow, slot_of(y + 2, zz))

    def to_home():
        @pl.when(zh != x)
        def _():
            remote(hop, hop, xsem.at[4], rsem.at[HOP, 0], partner).wait_recv()

        @pl.when(source)
        def _():
            own_hop.wait()

        slot = slot_of(y, x)

        @pl.when(home)
        def _():
            own_dr.start()

        @pl.when(zl != y)
        def _():
            remote(hop, dr.at[s, slot], xsem.at[5], rsem.at[DR, slot], at(y_=zl)).start()

    up = (zl >= y) & (zl < 3)
    down = (zl <= y) & (zl > 0)

    def along(d):
        slot = slot_of(y + d, x)
        if d == 0:

            @pl.when(home)
            def _():
                own_dr.wait()

            @pl.when(zl != y)
            def _():
                arrived(DR, slot)
        else:
            arrived(DR, slot)

        @pl.when(up)
        def _():
            send(DR, slot, at(zl_=zl + 1), sem=xsem.at[6])

        @pl.when(down)
        def _():
            send(DR, slot, at(zl_=zl - 1), sem=xsem.at[7])

        send(DR, slot, at(x_=x + 1))
        send(DR, slot, at(x_=x - 1))

    def x_near(d):
        for e in (-1, 1):
            slot = slot_of(y + d, x + e)
            arrived(DR, slot)
            send(DR, slot, at(x_=x - e), half=0 if e < 0 else 1)

    def x_far(d):
        arrived(DR, slot_of(y + d, x + 2))

    def nk_part(yy, u, half=None):
        first = 64 * lax.rem(yy + 4, 4) + 32 * u
        if half is None:
            return nk.at[pl.ds(first, 32), :]
        return nk.at[pl.ds(first + 16 * half, 16), :]

    def nk_sem(yy, u):
        return rsem.at[NK, 2 * lax.rem(yy + 4, 4) + u]

    def nk_send(yy, u, device, sem, half=None):
        part = nk_part(yy, u, half)
        remote(part, part, sem, nk_sem(yy, u), device).start()

    def nk_arrived(yy, u):
        part = nk_part(yy, u)
        remote(part, part, ssem.at[NK], nk_sem(yy, u), partner).wait_recv()

    def nk_own(u):
        @pl.when(top)
        def _():
            own_nk[u].wait()

        @pl.when(row != 0)
        def _():
            nk_arrived(y, u)

        @pl.when(zh != (3 if u == 0 else 1))
        def _():
            nk_send(y, u, at(zh_=zh + (1 if u == 0 else -1)), xsem.at[8 + u])

        nk_send(y, u, at(y_=y + 1), ssem.at[NK])
        nk_send(y, u, at(y_=y - 1), ssem.at[NK])

    def nk_near(u):
        for d in (-1, 1):
            nk_arrived(y + d, u)
            nk_send(y + d, u, at(y_=y - d), ssem.at[NK], half=0 if d < 0 else 1)

    @pl.when(top)
    def _():
        for t in (1, 3, 2):
            for u in range(2):
                src = normals.at[pl.ds(64 * t + 32 * u, 32), :]
                remote(src, nk_part(t, u), xsem.at[10], nk_sem(t, u), (4 * t, col)).start()

    def nr_part(xx, u):
        return nr.at[s, lax.rem(xx + 4, 4), pl.ds(48 * u, 48), :]

    def nr_sem(xx, u):
        return rsem.at[NR, 2 * lax.rem(xx + 4, 4) + u]

    def nr_send(xx, u, device, sem):
        part = nr_part(xx, u)
        remote(part, part, sem, nr_sem(xx, u), device).start()

    def nr_arrived(xx, u):
        part = nr_part(xx, u)
        remote(part, part, ssem.at[NR], nr_sem(xx, u), partner).wait_recv()

    def nr_own(u):
        @pl.when(side)
        def _():
            own_nr[u].wait()

        @pl.when(col != 0)
        def _():
            nr_arrived(x, u)

        @pl.when(zl < 3)
        def _():
            nr_send(x, u, at(zl_=zl + 1), xsem.at[11])

        nr_send(x, u, at(x_=x + 1), ssem.at[NR])
        nr_send(x, u, at(x_=x - 1), ssem.at[NR])

    def nr_near():
        for u in range(2):
            nr_arrived(x - 1, u)
            nr_arrived(x + 1, u)
            if u == 0:
                nr_send(x - 1, 0, at(x_=x + 1), ssem.at[NR])
            else:
                nr_send(x + 1, 1, at(x_=x - 1), ssem.at[NR])

    @pl.when(side)
    def _():
        for t in (2, 6, 1, 3, 7, 4, 5):
            h, q = t % 2, t // 2
            for u in range(2):
                src = normals.at[pl.ds(384 * h + 96 * q + 48 * u, 48), pl.ds(0, B)]
                dst = nr.at[h, q, pl.ds(48 * u, 48), :]
                remote(src, dst, xsem.at[12 + h], rsem.at[NR, 2 * q + u], (row, t)).start()

    def n0_send(q, device, sem):
        part = n0.at[s, q]
        remote(part, part, sem, rsem.at[N0, q], device).start()

    def n0_arrived(q):
        part = n0.at[s, q]
        remote(part, part, ssem.at[N0], rsem.at[N0, q], partner).wait_recv()

    def n0_own(level):
        if level == 0:

            @pl.when(top)
            def _():
                @pl.when(side)
                def _():
                    own_n0.wait()

                @pl.when(col != 0)
                def _():
                    n0_arrived(k)

                for d in (1, 3, 2):
                    n0_send(k, at(y_=y + d), xsem.at[14])
                n0_send(k, at(zh_=zh + 1), xsem.at[15])
                n0_send(k, at(zh_=zh - 1), xsem.at[15])
        elif level == 1:

            @pl.when((zh == 0) & (y != 0))
            def _():
                n0_arrived(k)
                n0_send(k, at(zh_=zh + 1), xsem.at[15])
                n0_send(k, at(zh_=zh - 1), xsem.at[15])
        elif level == 2:

            @pl.when(zh == 1)
            def _():
                n0_arrived(k)
                n0_send(k, at(zh_=zh + 1), xsem.at[16])

            @pl.when(zh == 3)
            def _():
                n0_arrived(k)
        else:

            @pl.when(zh == 2)
            def _():
                n0_arrived(k)

    def n0_plane(d):
        q = slot_of(zl + d, x)
        if d == 0:
            for e in (1, 2, 3):
                n0_send(q, at(zl_=zl + e), ssem.at[N0])
        else:
            n0_arrived(q)
        for e in (1, 3, 2):
            n0_send(q, at(x_=x + e), ssem.at[N0])

    def n0_rest(d):
        for e in (1, 2, 3):
            n0_arrived(slot_of(zl + d, x + e))

    def shared(which, h):
        if which < 4:
            part = dr.at[h, pl.ds(4 * lax.rem(y + which, 4), 4)]
        else:
            part = (d0, n0, nr)[which - 4].at[h]
        return remote(part, part, psem.at[which, 0], psem.at[which, 1], partner)

    def share(which):
        shared(which, s).start()

    far = lax.rem(x - zh + 4, 4) == 2
    off_home = lax.abs(zl - y)

    def only(condition, *steps):
        @pl.when(condition)
        def _():
            for step in steps:
                step[0](*step[1:])

    z_send(DK, design)
    y_send(DK, zh, design)
    own.wait()
    only(source, (to_home,))
    y_near(DK, zh)
    only(zh == 0, (nk_own, 0), (nk_own, 1))
    only(zl == 0, (nr_own, 0), (nr_own, 1))
    z_near(DK, -1)
    z_near(DK, 1)
    n0_own(0)

    @pl.when(col != 0)
    def _():
        arrived(D0, row)

    @pl.when(side)
    def _():
        own_corner.wait()

    z_send(D0)
    y_send(D0, zh)
    only(zl == 1, (nr_own, 0), (nr_own, 1))
    y_near(DK, zh - 1)
    y_near(DK, zh + 1)
    only((zh != x) & (lax.rem(x - zh + 4, 4) != 2), (to_home,))
    n0_own(1)
    only(zh == 1, (nk_own, 0))
    only(zh == 3, (nk_own, 1))
    only(zl == 2, (nr_own, 0), (nr_own, 1))
    z_near(D0, -1)
    z_near(D0, 1)
    z_far(DK)
    n0_own(2)
    only(zl == 3, (nr_own, 0), (nr_own, 1))
    only(far, (to_home,))
    only(zh == 2, (nk_own, 0), (nk_own, 1))
    y_near(DK, zh + 2)
    nr_near()
    z_far(D0)
    only(off_home == 0, *[(along, d) for d in (0, 1, 3, 2)])
    n0_own(3)
    n0_plane(0)
    only(zh == 3, (nk_own, 0))
    only(zh == 1, (nk_own, 1))
    only(off_home == 1, *[(along, d) for d in (0, 1, 3, 2)])
    for zz in (0, -1, 1, 2):
        y_far(D0, zh + zz)
    share(4)
    for d in (1, 3, 2):
        n0_plane(d)
    nk_near(0)
    nk_near(1)
    only(off_home == 2, *[(along, d) for d in (0, 1, 3, 2)])
    for d in (0, 1, 3, 2):
        n0_rest(d)
    share(5)
    nr_arrived(x + 2, 0)
    nr_arrived(x + 2, 1)
    share(6)
    only(off_home == 3, *[(along, d) for d in (0, 1, 3, 2)])
    for d in (0, 1, 3, 2):
        x_near(d)
    for zz in (0, -1, 1, 2):
        y_far(DK, zh + zz)
    nk_arrived(y + 2, 0)
    nk_arrived(y + 2, 1)
    for d in (0, 1, 3, 2):
        x_far(d)
        share(d)

    for which in range(7):
        shared(which, 1 - s).wait_recv()
    for which in range(7):
        shared(which, s).wait_send()

    def drained(part, flow):
        remote(part, part, ssem.at[flow], rsem.at[DK, 0], partner).wait_send()

    drained(dk.at[pl.ds(0, 15)], DK)
    drained(d0.at[0, pl.ds(0, 15)], D0)
    drained(dr.at[0, pl.ds(0, 12)], DR)
    drained(nk.at[pl.ds(0, 192), :], NK)
    drained(nr.at[0, pl.ds(0, 3)], NR)
    drained(n0.at[0, pl.ds(0, 15)], N0)

    @pl.when(side)
    def _():
        sent(d0.at[0, pl.ds(0, 15)], 0)
        sent(d0.at[1], 1)
        sent(nr.at[0, pl.ds(0, 3)], 12)
        sent(nr.at[1], 13)

    @pl.when(top & side)
    def _():
        sent(n0.at[0, pl.ds(0, 15)], 2)
        sent(n0.at[1], 3)

    @pl.when(source)
    def _():
        sent(dk.at[pl.ds(0, 3)], 4)

    @pl.when(zl != y)
    def _():
        sent(hop, 5)

    @pl.when(up)
    def _():
        sent(dk.at[pl.ds(0, 4)], 6)

    @pl.when(down)
    def _():
        sent(dk.at[pl.ds(0, 4)], 7)

    @pl.when(zh != 3)
    def _():
        sent(nk_part(0, 0), 8)

    @pl.when(zh != 1)
    def _():
        sent(nk_part(0, 0), 9)

    @pl.when(top)
    def _():
        sent(nk.at[pl.ds(0, 192), :], 10)
        sent(n0.at[0, pl.ds(0, 3)], 14)

    @pl.when(zl < 3)
    def _():
        sent(nr.at[0, 0], 11)

    @pl.when(zh == 0)
    def _():
        sent(n0.at[0, pl.ds(0, 2)], 15)

    @pl.when(zh == 1)
    def _():
        sent(n0.at[0, 0], 16)


def gather_all(design, normals):
    f32 = jnp.float32
    wide = design.shape[1]
    shapes = [
        (16, P_SIZE, wide),
        (2, 16, P_SIZE, wide),
        (2, 16, P_SIZE, 128),
        (B, wide),
        (2, 4, 96, B),
        (2, 16, 8, B),
    ]
    dma = pltpu.SemaphoreType.DMA
    return pl.pallas_call(
        comm_kernel,
        out_shape=[jax.ShapeDtypeStruct(shape, f32) for shape in shapes],
        in_specs=[pl.BlockSpec(memory_space=VMEM), pl.BlockSpec(memory_space=pl.ANY)],
        out_specs=[pl.BlockSpec(memory_space=VMEM)] * 6,
        scratch_shapes=[VMEM((P_SIZE, wide), f32), dma((6,)), dma((7, 16)), dma((17,)), dma((7, 2)), dma((9,))],
        compiler_params=pltpu.CompilerParams(collective_id=0, has_side_effects=True),
    )(design, normals)


def dot(a, b, da=1, db=0, precision=HIGHEST):
    return lax.dot_general(a, b, (((da,), (db,)), ((), ())), precision=precision, preferred_element_type=jnp.float32)


def split(a):
    high = a.astype(jnp.bfloat16)
    return high, (a - high.astype(jnp.float32)).astype(jnp.bfloat16)


def dot3(a, b, da=0, db=0):
    (ah, al), (bh, bl) = a, b
    return dot(ah, bh, da, db, None) + (dot(ah, bl, da, db, None) + dot(al, bh, da, db, None))


def iota(shape, dim):
    return lax.broadcasted_iota(jnp.int32, shape, dim)


def eliminate(block):
    nb = block.shape[0]
    wide = (8, 2 * nb)
    right = (iota((nb, nb), 0) == iota((nb, nb), 1)).astype(jnp.float32)
    rows = [jnp.concatenate([block[o : o + 8, :], right[o : o + 8, :]], axis=1) for o in range(0, nb, 8)]
    place = iota(wide, 0)
    done = []
    for g in range(nb // 8):
        t = 8 * g
        below = range(g + 1, nb // 8)
        lead = [jnp.broadcast_to(rows[g][j : j + 1, :], wide) for j in range(8)]
        pivots = {
            (j, c): jnp.broadcast_to(lead[j][:, t + c : t + c + 1], wide) for j in range(8) for c in range(j, 8)
        }
        weights = {(i, j): jnp.broadcast_to(rows[i][:, t + j : t + j + 1], wide) for i in below for j in range(8)}
        final = jnp.zeros(wide, jnp.float32)
        diag = jnp.ones(wide, jnp.float32)
        for j in range(8):
            inverse = 1.0 / pivots[j, j]
            for c in range(j + 1, 8):
                ratio = pivots[j, c] * inverse
                for d in range(c, 8):
                    pivots[c, d] = pivots[c, d] - ratio * pivots[j, d]
                lead[c] = lead[c] - ratio * lead[j]
                for i in below:
                    weights[i, c] = weights[i, c] - ratio * weights[i, j]
            scaled = lead[j] * inverse
            for i in below:
                rows[i] = rows[i] - weights[i, j] * scaled
            final = jnp.where(place == j, lead[j], final)
            diag = jnp.where(place == j, pivots[j, j], diag)
        done.append((final * (1.0 / jnp.sqrt(diag)))[:, nb:])
    return jnp.concatenate(done, axis=0)


def inverse_factor(a, w, n, nb):
    w[...] = (iota((n, n), 0) == iota((n, n), 1)).astype(jnp.float32)
    for o in range(0, n, nb):
        e = o + nb
        own = eliminate(a[o:e, o:e])
        left = dot(own, w[o:e, :e])
        w[o:e, :e] = left
        if e < n:
            right = dot(own, a[o:e, e:])
            a[e:, e:] -= dot(right, right, 0, 0)
            w[e:, :e] -= dot(right, left, 0, 0)


def compute_kernel(nb, normals, dk, dr, d0, nk, nr, n0, filters, regular, out, toeplitz, fk, fr, corner, inverse):
    row = lax.axis_index("row")
    col = lax.axis_index("col")
    rows, cols = normals.shape
    step = 4 * P_SIZE
    toeplitz[...] = jnp.zeros_like(toeplitz)
    for i in range(4):
        here = slice(P_SIZE * i, P_SIZE * (i + 1))
        toeplitz[here, P_SIZE * i : P_SIZE * (i + 1)] = filters[1]
        toeplitz[here, P_SIZE * (i + 1) : P_SIZE * (i + 2)] = filters[0]
    taps = toeplitz[...]

    def filtered(data):
        parts = [dot(taps[:, P_SIZE:], data[:step, :])]
        for o in range(step, OBS, step):
            parts.append(dot(taps, data[o - P_SIZE : o + step, :]))
        return jnp.concatenate(parts, axis=0)

    f0 = filtered(jnp.concatenate([d0[0], d0[1]], axis=1))
    reg0 = jnp.where(iota((B, B), 0) == iota((B, B), 1), regular[:, :B], 0.0)
    corner[...] = n0[...] + dot(f0, f0, 0, 0) + reg0
    inverse_factor(corner, inverse, B, nb)
    w = inverse[...]
    f0s = split(f0)
    fk[...] = filtered(dk)
    fks = split(fk[...])

    def strip(base, data, first, width):
        reg = regular[:, pl.ds(pl.multiple_of(first, 128), width)]
        same = iota((B, width), 0) == iota((B, width), 1) + first
        return base + dot3(f0s, data) + jnp.where(same, reg, 0.0)

    pk = dot(w, strip(nk[...], fks, cols * col, cols))
    pks = split(pk)
    half = rows // 2
    reg = regular[:, pl.ds(pl.multiple_of(cols * col, 128), cols)]
    for h in range(2):
        here = slice(half * h, half * (h + 1))
        first = row * rows + half * h
        fr[...] = filtered(dr.at[h])
        frs = split(fr[...])
        same = iota((half, B), 0) + first == iota((half, B), 1)
        pr = dot(nr[here, :] + dot3(frs, f0s) + jnp.where(same, regular[:, :B], 0.0), w, 1, 1)
        same = iota((half, cols), 0) + first == iota((half, cols), 1) + cols * col
        tile = normals[here, :] + jnp.where(same, reg, 0.0) + dot3(frs, fks)
        out[here, :] = tile - dot3(split(pr), pks, 1, 0)

        @pl.when(col == 0)
        def _():
            out[here, :B] = pr


def local_step(nb, normals, gathered, filters, regular):
    dk, dr, d0, nk, nr, n0 = gathered
    rows, cols = normals.shape
    f32 = jnp.float32
    return pl.pallas_call(
        functools.partial(compute_kernel, nb),
        out_shape=jax.ShapeDtypeStruct((rows, cols), f32),
        in_specs=[pl.BlockSpec(memory_space=VMEM)] * 9,
        out_specs=pl.BlockSpec(memory_space=VMEM),
        scratch_shapes=[
            VMEM((4 * P_SIZE, 5 * P_SIZE), f32),
            VMEM((OBS, cols), f32),
            VMEM((OBS, cols), f32),
            VMEM((B, B), f32),
            VMEM((B, B), f32),
        ],
    )(
        normals,
        dk.reshape(OBS, cols),
        dr.reshape(2, OBS, cols),
        d0.reshape(2, OBS, 128),
        nk,
        nr.reshape(rows, B),
        n0.reshape(B, B),
        filters,
        regular.reshape(1, -1),
    )


def body(normals, design, filter_blocks, regular):
    gathered = gather_all(design, normals)
    return local_step(128, normals, gathered, filter_blocks, regular)


def solution(mesh):
    in_specs = (P("row", "col"), P("row", "col"), P(), P())
    out_specs = P("row", "col")
    return jax.shard_map(body, mesh=mesh, in_specs=in_specs, out_specs=out_specs, check_vma=False)
```

time: 1250 us -> 89.2 us (0.07)
  waiting for transfers between devices: 1080 us -> 0 us
  Pallas kernels: 0 us -> 88.5 us
  other arithmetic: 59.4 us -> 0 us
  blocking collectives: 58.6 us -> 0 us
  between operations: 14.7 us -> 0.01 us
    psum x4 -> x0, waiting for transfers between devices: 1080 us -> none  [broadcast(): return lax.psum(block, axis)]
    pallas_call x0 -> x2, Pallas kernels: none -> 88.5 us  [the longest x1 64.8 us: gather_all(): pl.pallas_call(comm_kernel, out_shape=[jax.ShapeDtypeStruct(shape, f32) f...]
    all_gather x1 -> x0, blocking collectives: 58.6 us -> none  [body(): columns = lax.all_gather(filtered, 'row', axis=0, tiled=True)]
    another operation x9 -> x0, other arithmetic: 53.7 us -> none  [the longest x6 34 us: body(): factor = jnp.linalg.cholesky(corner)]
  transfers between devices with their start and end apart: 5 -> 0, of which waited for: 5 -> 0; matrix products, arithmetic and copies ran while one was open for 0% -> 0% of each run, Pallas kernels for 0% -> 0%
where the time goes in v2:
time: 89.2 us; the launch traced here: 88.5 us
  Pallas kernels  88.5 us (99%)
    pallas_call x1, Pallas kernels, gather_all(): pl.pallas_call(comm_kernel, out_shape=[jax.ShapeDtypeStruct(shape, f32) f...  64.8 us
    pallas_call x1, Pallas kernels, local_step(): pl.pallas_call(functools.partial(compute_kernel, nb), out_shape=jax.Shape...  23.8 us

profile of v2, /device:TPU:24, one launch (start us, length us, event | category | flops | bytes accessed | tf_op | source)
XLA Modules:
  0.0 88.5 jit_solution(2480355312836721312)
XLA Ops:
  0.0 64.8 %shard_map.46 = (f32[16,32,384]{2,1,0:T(8,128)}, f32[2,16,32,384]{3,2,1,0:T(8,128)}, f32[2,16,32,128]{3,2,1,0:T(8,128)}, f32[256,384]{1,0:T(8,128)}, f32[2,4,96,...) custom-call(f32[32,384]{1,0:T(8,128)} %design.1, f32[768,384]{1,0:T(8,128)} %normals.3), custom_call_target="tpu_custom_call" | custom-call | tf_op jit(solution)/shard_map/pallas_call | solution.py:558
  64.8 23.8 %shard_map.47 = f32[768,384]{1,0:T(8,128)} custom-call(f32[768,384]{1,0:T(8,128)} %normals.3, f32[512,384]{1,0:T(8,128)} %bitcast.7, f32[2,512,384]{2,1,0:T(8,128)} %bitcast.6, f32[2,512,128]{2,1,0:T(8,128)} %bitcast.9, f32[256,384]{1,0:T(8,128)} %get-tuple-element.14.nk, f32[768,256]{1,0:T(8,128)} %bitcast.8, f32[256,256]{1,0:T(8,128)} %bitcast.10, ...), custom_call_target="tpu_custom_call" | custom-call | tf_op jit(solution)/shard_map/pallas_call | solution.py:690

commit v3 on v2

--- a/solution.py
+++ b/solution.py
@@ -17,7 +17,9 @@
 DK, D0, NK, N0, DR, NR, HOP = range(7)
 
 
-def comm_kernel(design, normals, dk, dr, d0, nk, nr, n0, hop, ssem, rsem, xsem, psem, lsem):
+def kernel(design, normals, filters, regular, out, *scratch):
+    (dk, dr, d0, nk, nr, n0, hop, ssem, rsem, xsem, psem, lsem) = scratch[:12]
+    (tile, result, toeplitz, f0, fk, fr, corner, inverse) = scratch[12:]
     row = lax.axis_index("row")
     col = lax.axis_index("col")
     s = lax.rem(col, 2)
@@ -62,6 +64,8 @@
 
     own = copy(design, dk.at[row], 0)
     own.start()
+    own_tile = copy(normals, tile, 9)
+    own_tile.start()
     own_hop = copy(design, hop, 1)
     own_corner = copy(design.at[:, pl.ds(0, 128)], d0.at[0, row], 2)
     own_n0 = copy(normals.at[pl.ds(0, 8), pl.ds(0, B)], n0.at[0, 0], 3)
@@ -448,34 +452,102 @@
     n0_plane(0)
     only(zh == 3, (nk_own, 0))
     only(zh == 1, (nk_own, 1))
-    only(off_home == 1, *[(along, d) for d in (0, 1, 3, 2)])
     for zz in (0, -1, 1, 2):
         y_far(D0, zh + zz)
     share(4)
+    only(off_home == 1, *[(along, d) for d in (0, 1, 3, 2)])
     for d in (1, 3, 2):
         n0_plane(d)
-    nk_near(0)
-    nk_near(1)
-    only(off_home == 2, *[(along, d) for d in (0, 1, 3, 2)])
     for d in (0, 1, 3, 2):
         n0_rest(d)
     share(5)
-    nr_arrived(x + 2, 0)
-    nr_arrived(x + 2, 1)
-    share(6)
-    only(off_home == 3, *[(along, d) for d in (0, 1, 3, 2)])
-    for d in (0, 1, 3, 2):
-        x_near(d)
-    for zz in (0, -1, 1, 2):
-        y_far(DK, zh + zz)
-    nk_arrived(y + 2, 0)
-    nk_arrived(y + 2, 1)
-    for d in (0, 1, 3, 2):
+    nk_near(0)
+    nk_near(1)
+    shared(4, 1 - s).wait_recv()
+
+    def nr_far():
+        nr_arrived(x + 2, 0)
+        nr_arrived(x + 2, 1)
+        share(6)
+
+    def nk_far():
+        nk_arrived(y + 2, 0)
+        nk_arrived(y + 2, 1)
+
+    def x_last(d):
         x_far(d)
         share(d)
 
-    for which in range(7):
-        shared(which, 1 - s).wait_recv()
+    steps = [(lambda: only(off_home == 2, *[(along, d) for d in (0, 1, 3, 2)]))]
+    steps += [nr_far, (lambda: only(off_home == 3, *[(along, d) for d in (0, 1, 3, 2)]))]
+    steps += [functools.partial(x_near, d) for d in (0, 1, 3, 2)]
+    steps += [functools.partial(y_far, DK, zh + zz) for zz in (0, -1, 1, 2)]
+    steps += [nk_far] + [functools.partial(x_last, d) for d in (0, 1, 3, 2)]
+    turn = [0]
+
+    def tick():
+        turn[0] += 1
+        if turn[0] % 2 == 0 and steps:
+            steps.pop(0)()
+
+    rows, cols = tile.shape
+    half = rows // 2
+    toeplitz[...] = jnp.zeros_like(toeplitz)
+    for i in range(4):
+        here = slice(P_SIZE * i, P_SIZE * (i + 1))
+        toeplitz[here, P_SIZE * i : P_SIZE * (i + 1)] = filters[1]
+        toeplitz[here, P_SIZE * (i + 1) : P_SIZE * (i + 2)] = filters[0]
+
+    def filtered(load, dst):
+        width = dst.shape[1]
+        for q in range(0, 16, 4):
+            first = max(q - 1, 0)
+            data = load(first, q + 4).reshape(P_SIZE * (q + 4 - first), width)
+            taps = toeplitz[:, P_SIZE:] if q == 0 else toeplitz[...]
+            dst[P_SIZE * q : P_SIZE * (q + 4), :] = dot(taps, data)
+
+    filtered(lambda a, b: jnp.concatenate([d0[0, a:b], d0[1, a:b]], axis=2), f0)
+    gram = dot(f0[...], f0[...], 0, 0)
+    steps.pop(0)()
+    shared(5, 1 - s).wait_recv()
+    reg0 = jnp.where(iota((B, B), 0) == iota((B, B), 1), regular[:, :B], 0.0)
+    corner[...] = n0[...].reshape(B, B) + gram + reg0
+    inverse_factor(corner, inverse, B, 128, tick)
+    while steps:
+        steps.pop(0)()
+    w = inverse[...]
+    f0s = split(f0[...])
+    filtered(lambda a, b: dk[a:b], fk)
+    fks = split(fk[...])
+    reg = regular[:, pl.ds(pl.multiple_of(cols * col, 128), cols)]
+    same = iota((B, cols), 0) == iota((B, cols), 1) + cols * col
+    pks = split(dot(w, nk[...] + dot3(f0s, fks) + jnp.where(same, reg, 0.0)))
+    own_tile.wait()
+    shared(6, 1 - s).wait_recv()
+    flush = []
+    for e in range(2):
+        h = s if e == 0 else 1 - s
+        if e == 1:
+            for which in range(4):
+                shared(which, h).wait_recv()
+        filtered(lambda a, b: dr[h, a:b], fr)
+        frs = split(fr[...])
+        first = row * rows + half * h
+        same = iota((half, B), 0) + first == iota((half, B), 1)
+        strip = nr[h].reshape(half, B) + dot3(frs, f0s) + jnp.where(same, regular[:, :B], 0.0)
+        pr = dot(strip, w, 1, 1)
+        here = pl.ds(pl.multiple_of(half * h, 8), half)
+        same = iota((half, cols), 0) + first == iota((half, cols), 1) + cols * col
+        value = tile[here, :] + jnp.where(same, reg, 0.0) + dot3(frs, fks)
+        result[e] = value - dot3(split(pr), pks, 1, 0)
+
+        @pl.when(side)
+        def _():
+            result[e, :, :B] = pr
+
+        flush.append(copy(result.at[e], out.at[here, :], 10 + e))
+        flush[e].start()
+
     for which in range(7):
         shared(which, s).wait_send()
 
@@ -542,27 +614,26 @@
     def _():
         sent(n0.at[0, 0], 16)
 
-
-def gather_all(design, normals):
+    flush[0].wait()
+    flush[1].wait()
+
+
+def local_step(normals, design, filters, regular):
     f32 = jnp.float32
-    wide = design.shape[1]
-    shapes = [
-        (16, P_SIZE, wide),
-        (2, 16, P_SIZE, wide),
-        (2, 16, P_SIZE, 128),
-        (B, wide),
-        (2, 4, 96, B),
-        (2, 16, 8, B),
-    ]
+    rows, cols = normals.shape
     dma = pltpu.SemaphoreType.DMA
+    blocks = [(16, P_SIZE, cols), (2, 16, P_SIZE, cols), (2, 16, P_SIZE, 128), (B, cols), (2, 4, 96, B), (2, 16, 8, B)]
+    blocks += [(P_SIZE, cols)]
+    sems = [dma((6,)), dma((7, 16)), dma((17,)), dma((7, 2)), dma((12,))]
+    work = [(rows, cols), (2, rows // 2, cols), (4 * P_SIZE, 5 * P_SIZE), (OBS, B), (OBS, cols), (OBS, cols), (B, B), (B, B)]
     return pl.pallas_call(
-        comm_kernel,
-        out_shape=[jax.ShapeDtypeStruct(shape, f32) for shape in shapes],
-        in_specs=[pl.BlockSpec(memory_space=VMEM), pl.BlockSpec(memory_space=pl.ANY)],
-        out_specs=[pl.BlockSpec(memory_space=VMEM)] * 6,
-        scratch_shapes=[VMEM((P_SIZE, wide), f32), dma((6,)), dma((7, 16)), dma((17,)), dma((7, 2)), dma((9,))],
+        kernel,
+        out_shape=jax.ShapeDtypeStruct((rows, cols), f32),
+        in_specs=[pl.BlockSpec(memory_space=space) for space in (VMEM, pl.ANY, VMEM, VMEM)],
+        out_specs=pl.BlockSpec(memory_space=pl.ANY),
+        scratch_shapes=[VMEM(shape, f32) for shape in blocks] + sems + [VMEM(shape, f32) for shape in work],
         compiler_params=pltpu.CompilerParams(collective_id=0, has_side_effects=True),
-    )(design, normals)
+    )(design, normals, filters, regular.reshape(1, -1))
 
 
 def dot(a, b, da=1, db=0, precision=HIGHEST):
@@ -583,7 +654,7 @@
     return lax.broadcasted_iota(jnp.int32, shape, dim)
 
 
-def eliminate(block):
+def eliminate(block, tick):
     nb = block.shape[0]
     wide = (8, 2 * nb)
     right = (iota((nb, nb), 0) == iota((nb, nb), 1)).astype(jnp.float32)
@@ -615,14 +686,15 @@
             final = jnp.where(place == j, lead[j], final)
             diag = jnp.where(place == j, pivots[j, j], diag)
         done.append((final * (1.0 / jnp.sqrt(diag)))[:, nb:])
+        tick()
     return jnp.concatenate(done, axis=0)
 
 
-def inverse_factor(a, w, n, nb):
+def inverse_factor(a, w, n, nb, tick):
     w[...] = (iota((n, n), 0) == iota((n, n), 1)).astype(jnp.float32)
     for o in range(0, n, nb):
         e = o + nb
-        own = eliminate(a[o:e, o:e])
+        own = eliminate(a[o:e, o:e], tick)
         left = dot(own, w[o:e, :e])
         w[o:e, :e] = left
         if e < n:
@@ -631,90 +703,8 @@
             w[e:, :e] -= dot(right, left, 0, 0)
 
 
-def compute_kernel(nb, normals, dk, dr, d0, nk, nr, n0, filters, regular, out, toeplitz, fk, fr, corner, inverse):
-    row = lax.axis_index("row")
-    col = lax.axis_index("col")
-    rows, cols = normals.shape
-    step = 4 * P_SIZE
-    toeplitz[...] = jnp.zeros_like(toeplitz)
-    for i in range(4):
-        here = slice(P_SIZE * i, P_SIZE * (i + 1))
-        toeplitz[here, P_SIZE * i : P_SIZE * (i + 1)] = filters[1]
-        toeplitz[here, P_SIZE * (i + 1) : P_SIZE * (i + 2)] = filters[0]
-    taps = toeplitz[...]
-
-    def filtered(data):
-        parts = [dot(taps[:, P_SIZE:], data[:step, :])]
-        for o in range(step, OBS, step):
-            parts.append(dot(taps, data[o - P_SIZE : o + step, :]))
-        return jnp.concatenate(parts, axis=0)
-
-    f0 = filtered(jnp.concatenate([d0[0], d0[1]], axis=1))
-    reg0 = jnp.where(iota((B, B), 0) == iota((B, B), 1), regular[:, :B], 0.0)
-    corner[...] = n0[...] + dot(f0, f0, 0, 0) + reg0
-    inverse_factor(corner, inverse, B, nb)
-    w = inverse[...]
-    f0s = split(f0)
-    fk[...] = filtered(dk)
-    fks = split(fk[...])
-
-    def strip(base, data, first, width):
-        reg = regular[:, pl.ds(pl.multiple_of(first, 128), width)]
-        same = iota((B, width), 0) == iota((B, width), 1) + first
-        return base + dot3(f0s, data) + jnp.where(same, reg, 0.0)
-
-    pk = dot(w, strip(nk[...], fks, cols * col, cols))
-    pks = split(pk)
-    half = rows // 2
-    reg = regular[:, pl.ds(pl.multiple_of(cols * col, 128), cols)]
-    for h in range(2):
-        here = slice(half * h, half * (h + 1))
-        first = row * rows + half * h
-        fr[...] = filtered(dr.at[h])
-        frs = split(fr[...])
-        same = iota((half, B), 0) + first == iota((half, B), 1)
-        pr = dot(nr[here, :] + dot3(frs, f0s) + jnp.where(same, regular[:, :B], 0.0), w, 1, 1)
-        same = iota((half, cols), 0) + first == iota((half, cols), 1) + cols * col
-        tile = normals[here, :] + jnp.where(same, reg, 0.0) + dot3(frs, fks)
-        out[here, :] = tile - dot3(split(pr), pks, 1, 0)
-
-        @pl.when(col == 0)
-        def _():
-            out[here, :B] = pr
-
-
-def local_step(nb, normals, gathered, filters, regular):
-    dk, dr, d0, nk, nr, n0 = gathered
-    rows, cols = normals.shape
-    f32 = jnp.float32
-    return pl.pallas_call(
-        functools.partial(compute_kernel, nb),
-        out_shape=jax.ShapeDtypeStruct((rows, cols), f32),
-        in_specs=[pl.BlockSpec(memory_space=VMEM)] * 9,
-        out_specs=pl.BlockSpec(memory_space=VMEM),
-        scratch_shapes=[
-            VMEM((4 * P_SIZE, 5 * P_SIZE), f32),
-            VMEM((OBS, cols), f32),
-            VMEM((OBS, cols), f32),
-            VMEM((B, B), f32),
-            VMEM((B, B), f32),
-        ],
-    )(
-        normals,
-        dk.reshape(OBS, cols),
-        dr.reshape(2, OBS, cols),
-        d0.reshape(2, OBS, 128),
-        nk,
-        nr.reshape(rows, B),
-        n0.reshape(B, B),
-        filters,
-        regular.reshape(1, -1),
-    )
-
-
 def body(normals, design, filter_blocks, regular):
-    gathered = gather_all(design, normals)
-    return local_step(128, normals, gathered, filter_blocks, regular)
+    return local_step(normals, design, filter_blocks, regular)
 
 
 def solution(mesh):

time: 89.2 us -> 81.7 us (0.916)
  Pallas kernels: 88.5 us -> 79.2 us
  local copies, waits for them, and re-layouts: 0 us -> 2.36 us
    pallas_call x2 -> x1, Pallas kernels: 88.5 us -> 79.2 us  [local_step(): pl.pallas_call(kernel, out_shape=jax.ShapeDtypeStruct((rows, cols), f32),...]
    unnamed x0 -> x1, local copies, waits for them, and re-layouts: none -> 2.36 us
where the time goes in v3:
time: 81.7 us; the launch traced here: 81.5 us
  Pallas kernels  79.2 us (97%)
  local copies, waits for them, and re-layouts  2.36 us (3%)
    pallas_call x1, Pallas kernels, local_step(): pl.pallas_call(kernel, out_shape=jax.ShapeDtypeStruct((rows, cols), f32),...  79.2 us
    unnamed x1, local copies, waits for them, and re-layouts  2.36 us

profile of v3, /device:TPU:24, one launch (start us, length us, event | category | flops | bytes accessed | tf_op | source)
XLA Modules:
  0.0 81.5 jit_solution(13736427785526327109)
XLA Ops:
  0.0 79.2 %shard_map.46 = f32[768,384]{1,0:T(8,128)} custom-call(f32[32,384]{1,0:T(8,128)} %design.1, f32[768,384]{1,0:T(8,128)} %normals.1, f32[2,32,32]{2,1,0:T(8,128)} %filters.1, f32[1,12288]{1,0:T(1,128)} %bitcast.1), custom_call_target="tpu_custom_call" | custom-call | tf_op jit(solution)/shard_map/pallas_call | solution.py:629
  79.2 2.4 %copy.6 = f32[768,384]{1,0:T(8,128)} copy(f32[768,384]{1,0:T(8,128)} %shard_map.46) | data formatting | bytes 2359296

commit v4 on v3

--- a/solution.py
+++ b/solution.py
@@ -413,51 +413,51 @@
     own.wait()
     only(source, (to_home,))
     y_near(DK, zh)
+
+    @pl.when(col != 0)
+    def _():
+        arrived(D0, row)
+
+    @pl.when(side)
+    def _():
+        own_corner.wait()
+
+    z_send(D0)
+    y_send(D0, zh)
+    n0_own(0)
     only(zh == 0, (nk_own, 0), (nk_own, 1))
     only(zl == 0, (nr_own, 0), (nr_own, 1))
     z_near(DK, -1)
     z_near(DK, 1)
-    n0_own(0)
-
-    @pl.when(col != 0)
-    def _():
-        arrived(D0, row)
-
-    @pl.when(side)
-    def _():
-        own_corner.wait()
-
-    z_send(D0)
-    y_send(D0, zh)
+    n0_own(1)
     only(zl == 1, (nr_own, 0), (nr_own, 1))
     y_near(DK, zh - 1)
     y_near(DK, zh + 1)
     only((zh != x) & (lax.rem(x - zh + 4, 4) != 2), (to_home,))
-    n0_own(1)
+    z_near(D0, -1)
+    z_near(D0, 1)
+    n0_own(2)
     only(zh == 1, (nk_own, 0))
     only(zh == 3, (nk_own, 1))
     only(zl == 2, (nr_own, 0), (nr_own, 1))
-    z_near(D0, -1)
-    z_near(D0, 1)
     z_far(DK)
-    n0_own(2)
+    only(far, (to_home,))
+    z_far(D0)
+    n0_own(3)
+    n0_plane(0)
     only(zl == 3, (nr_own, 0), (nr_own, 1))
-    only(far, (to_home,))
     only(zh == 2, (nk_own, 0), (nk_own, 1))
     y_near(DK, zh + 2)
-    nr_near()
-    z_far(D0)
     only(off_home == 0, *[(along, d) for d in (0, 1, 3, 2)])
-    n0_own(3)
-    n0_plane(0)
-    only(zh == 3, (nk_own, 0))
-    only(zh == 1, (nk_own, 1))
+    for d in (1, 3, 2):
+        n0_plane(d)
     for zz in (0, -1, 1, 2):
         y_far(D0, zh + zz)
     share(4)
+    only(zh == 3, (nk_own, 0))
+    only(zh == 1, (nk_own, 1))
+    nr_near()
     only(off_home == 1, *[(along, d) for d in (0, 1, 3, 2)])
-    for d in (1, 3, 2):
-        n0_plane(d)
     for d in (0, 1, 3, 2):
         n0_rest(d)
     share(5)
@@ -481,7 +481,6 @@
     steps = [(lambda: only(off_home == 2, *[(along, d) for d in (0, 1, 3, 2)]))]
     steps += [nr_far, (lambda: only(off_home == 3, *[(along, d) for d in (0, 1, 3, 2)]))]
     steps += [functools.partial(x_near, d) for d in (0, 1, 3, 2)]
-    steps += [functools.partial(y_far, DK, zh + zz) for zz in (0, -1, 1, 2)]
     steps += [nk_far] + [functools.partial(x_last, d) for d in (0, 1, 3, 2)]
     turn = [0]
 
@@ -509,6 +508,9 @@
     filtered(lambda a, b: jnp.concatenate([d0[0, a:b], d0[1, a:b]], axis=2), f0)
     gram = dot(f0[...], f0[...], 0, 0)
     steps.pop(0)()
+    for zz in (0, -1, 1, 2):
+        y_far(DK, zh + zz)
+    filtered(lambda a, b: dk[a:b], fk)
     shared(5, 1 - s).wait_recv()
     reg0 = jnp.where(iota((B, B), 0) == iota((B, B), 1), regular[:, :B], 0.0)
     corner[...] = n0[...].reshape(B, B) + gram + reg0
@@ -517,7 +519,6 @@
         steps.pop(0)()
     w = inverse[...]
     f0s = split(f0[...])
-    filtered(lambda a, b: dk[a:b], fk)
     fks = split(fk[...])
     reg = regular[:, pl.ds(pl.multiple_of(cols * col, 128), cols)]
     same = iota((B, cols), 0) == iota((B, cols), 1) + cols * col

time: 81.7 us -> 76.2 us (0.933)
  Pallas kernels: 79.2 us -> 73.3 us
    pallas_call x1, Pallas kernels: 79.2 us -> 73.3 us  [local_step(): pl.pallas_call(kernel, out_shape=jax.ShapeDtypeStruct((rows, cols), f32),...]
where the time goes in v4:
time: 76.2 us; the launch traced here: 75.7 us
  Pallas kernels  73.3 us (96%)
  local copies, waits for them, and re-layouts  2.36 us (3%)
    pallas_call x1, Pallas kernels, local_step(): pl.pallas_call(kernel, out_shape=jax.ShapeDtypeStruct((rows, cols), f32),...  73.3 us
    unnamed x1, local copies, waits for them, and re-layouts  2.36 us

profile of v4, /device:TPU:24, one launch (start us, length us, event | category | flops | bytes accessed | tf_op | source)
XLA Modules:
  0.0 75.7 jit_solution(3757847043292251122)
XLA Ops:
  0.0 73.3 %shard_map.46 = f32[768,384]{1,0:T(8,128)} custom-call(f32[32,384]{1,0:T(8,128)} %design.1, f32[768,384]{1,0:T(8,128)} %normals.1, f32[2,32,32]{2,1,0:T(8,128)} %filters.1, f32[1,12288]{1,0:T(1,128)} %bitcast.1), custom_call_target="tpu_custom_call" | custom-call | tf_op jit(solution)/shard_map/pallas_call | solution.py:630
  73.3 2.4 %copy.6 = f32[768,384]{1,0:T(8,128)} copy(f32[768,384]{1,0:T(8,128)} %shard_map.46) | data formatting | bytes 2359296
